TPU v7x, 256 devices: a whole 4x4x8 slice. The times are simulated.
256 devices in a mesh: dp: 64 (over z, x, y_hi), tensor: 4 (over y_lo, core).
Axes of the slice: x: 4, y: 4 (y_hi: 2, y_lo: 2; y = y_hi * 2 + y_lo), z: 8, core: 2. Of those that a mesh axis runs over, the one named last changes fastest.
Arguments:
- d_out: bfloat16 [16384, 3072], P('dp'), may hold values from -12 to 12
- gate: bfloat16 [16384, 4096], P('dp', 'tensor'), may hold values from -16 to 16
- up_proj: bfloat16 [16384, 4096], P('dp', 'tensor'), may hold values from -12 to 12
- master: float32 [4096, 3072], P(('tensor', 'dp')), may hold values from -0.09375 to 0.09375
- moment_one: float32 [4096, 3072], P(('tensor', 'dp')), may hold values from -4 to 4
- moment_two: float32 [4096, 3072], P(('tensor', 'dp')), may hold values from 0.05 to 2
Outputs:
- gate_grad: bfloat16 [16384, 4096], P('dp', 'tensor')
- up_grad: bfloat16 [16384, 4096], P('dp', 'tensor')
- master_next: float32 [4096, 3072], P(('tensor', 'dp'))
- moment_one_next: float32 [4096, 3072], P(('tensor', 'dp'))
- moment_two_next: float32 [4096, 3072], P(('tensor', 'dp'))
- weight_next: bfloat16 [4096, 3072], P('tensor')
All inputs are finite; a program needn't handle non-finite values.
Results may differ from a plain program's by a relative error of at most 0.005.
Values may be sent and summed in bfloat16 or wider, within the bound.
A program may use at most 64 MiB of HBM per device.

v0:
```python
import jax
import jax.numpy as jnp
from jax import lax
from jax.sharding import PartitionSpec as P

D = 3072
FF = 4096


def on_device(d_out, gate, up_proj, master, moment_one, moment_two):
    weight = master.astype(jnp.bfloat16)
    gate_f = gate.astype(jnp.float32)
    up_f = up_proj.astype(jnp.float32)
    silu_gate = jax.nn.silu(gate_f)
    hidden = (silu_gate * up_f).astype(jnp.bfloat16)
    d_hidden = lax.dot_general(
        d_out,
        lax.all_gather(weight, "dp", axis=0, tiled=True),
        (((1,), (1,)), ((), ())),
        preferred_element_type=jnp.float32,
    )
    partial_term = lax.dot_general(
        hidden, d_out, (((0,), (0,)), ((), ())), preferred_element_type=jnp.float32
    )
    grad = lax.psum_scatter(partial_term, "dp", scatter_dimension=0, tiled=True)
    up_grad = (d_hidden * silu_gate).astype(jnp.bfloat16)
    sigm = jax.nn.sigmoid(gate_f)
    gate_grad = (d_hidden * up_f * sigm * (1.0 + gate_f * (1.0 - sigm))).astype(jnp.bfloat16)
    local_squares = jnp.sum(grad * grad)
    total = lax.psum(local_squares, ("dp", "tensor"))
    factor = 1.0 / jnp.sqrt(total / (FF * D) + 1e-06)
    clipped = grad * factor
    moment_one_next = 0.9 * moment_one + 0.1 * clipped
    moment_two_next = 0.95 * moment_two + 0.05 * clipped * clipped
    master_next = master - 0.003 * (
        moment_one_next / (jnp.sqrt(moment_two_next) + 1e-08) + 0.1 * master
    )
    shard_next = master_next.astype(jnp.bfloat16)
    weight_next = lax.all_gather(shard_next, "dp", axis=0, tiled=True)
    return (gate_grad, up_grad, master_next, moment_one_next, moment_two_next, weight_next)


def solution(mesh):
    placed = (
        P("dp", None),
        P("dp", "tensor"),
        P("dp", "tensor"),
        P(("tensor", "dp"), None),
        P(("tensor", "dp"), None),
        P(("tensor", "dp"), None),
    )
    return jax.shard_map(
        on_device,
        mesh=mesh,
        in_specs=placed,
        out_specs=(
            P("dp", "tensor"),
            P("dp", "tensor"),
            P(("tensor", "dp"), None),
            P(("tensor", "dp"), None),
            P(("tensor", "dp"), None),
            P("tensor", None),
        ),
        check_vma=False,
    )
```

profile of v0, /device:TPU:2, one launch (start us, length us, event | category | flops | bytes accessed | tf_op | source)
XLA Modules:
  0.0 1212.7 jit_solution(3031577703967708781)
XLA Ops:
  7.2 0.0 copy-start
  7.2 0.0 reduce-scatter.2.cloned.1.call-start
  7.2 1.4 copy-done
  8.6 7.7 fusion.8
  16.3 0.0 copy-start.3
  16.3 0.0 copy-start.4
  16.3 0.0 copy-start.5
  16.3 0.0 copy-start.1
  16.3 0.0 copy-start.2
  16.3 0.0 reduce-scatter.2.cloned.1.call-update
  16.3 0.0 all-gather.3.cloned.1.call-start
  16.4 833.1 %reduce-scatter.2.cloned.1.call-done = f32[16,3072]{1,0:T(8,128)} async-done(((f32[1024,3072]{1,0:T(8,128)}), f32[16,3072]{1,0:T(8,128)}) %reduce-scatter.2.cloned.1.call-update) | async-done | bytes 196624 | tf_op jit(solution)/shard_map/reduce_scatter | solution.py:25
  849.5 1.6 multiply_reduce_fusion
  851.1 72.7 %psum.7 = f32[]{:T(128)} all-reduce(f32[]{:T(128)} %multiply_reduce_fusion), channel_id=1, replica_groups=mesh['dp'=64,'tensor'=4] {'dp','tensor'}, use_global_device_ids=true, to_apply=%region_2.3 | all-reduce | flops 1 | bytes 8 | tf_op jit(solution)/shard_map/psum | solution.py:30
  924.4 0.0 copy-done.3
  924.4 0.0 copy-done.4
  924.4 0.0 copy-done.5
  924.5 1.9 fusion.12
  926.3 0.0 all-gather.3.cloned.1.call-update
  926.3 0.0 all-gather.5.cloned.1.call-start
  926.4 0.7 all-gather.5.cloned.1.call-update
  927.1 134.7 %all-gather.3.cloned.1.call-done = bf16[1024,3072]{1,0:T(8,128)(2,1)} async-done(((bf16[16,3072]{1,0:T(8,128)(2,1)}), bf16[1024,3072]{1,0:T(8,128)(2,1)}) %all-gather.3.cloned.1.call-update) | async-done | bytes 6291472 | tf_op jit(solution)/shard_map/all_gather | solution.py:18
  1061.7 0.0 copy-done.1
  1061.7 0.0 copy-done.2
  1061.7 5.9 multiply_convert_fusion
  1067.6 132.6 %all-gather.5.cloned.1.call-done = bf16[1024,3072]{1,0:T(8,128)(2,1)} async-done(((bf16[16,3072]{1,0:T(8,128)(2,1)}), bf16[1024,3072]{1,0:T(8,128)(2,1)}) %all-gather.5.cloned.1.call-update) | async-done | bytes 6291472 | tf_op jit(solution)/shard_map/all_gather | solution.py:39
  1200.2 5.9 copy.13
Async XLA Ops:
  7.2 1.4 copy-start
  7.2 842.3 %reduce-scatter.2.cloned.1.call-start = ((), (), s32[]{:S(2)}) async-start(), calls=%async_computation.2 | async-start | bytes 12779520 | tf_op jit(solution)/shard_map/reduce_scatter | solution.py:25
  16.3 908.2 %copy-start.3 = (f32[16,3072]{1,0:T(8,128)S(1)}, f32[16,3072]{1,0:T(8,128)}, u32[]{:S(2)}) copy-start(f32[16,3072]{1,0:T(8,128)} %param.9) | copy-start | bytes 589828
  16.3 908.2 %copy-start.4 = (f32[16,3072]{1,0:T(8,128)S(1)}, f32[16,3072]{1,0:T(8,128)}, u32[]{:S(2)}) copy-start(f32[16,3072]{1,0:T(8,128)} %param.11) | copy-start | bytes 589828
  16.3 908.2 %copy-start.5 = (f32[16,3072]{1,0:T(8,128)S(1)}, f32[16,3072]{1,0:T(8,128)}, u32[]{:S(2)}) copy-start(f32[16,3072]{1,0:T(8,128)} %param.10) | copy-start | bytes 589828
  16.3 1045.5 %copy-start.1 = (bf16[256,1024]{1,0:T(8,128)(2,1)S(1)}, bf16[256,1024]{1,0:T(8,128)(2,1)}, u32[]{:S(2)}) copy-start(bf16[256,1024]{1,0:T(8,128)(2,1)} %param.7) | copy-start | bytes 1572868
  16.3 1045.5 %copy-start.2 = (bf16[256,1024]{1,0:T(8,128)(2,1)S(1)}, bf16[256,1024]{1,0:T(8,128)(2,1)}, u32[]{:S(2)}) copy-start(bf16[256,1024]{1,0:T(8,128)(2,1)} %param.8) | copy-start | bytes 1572868
  16.3 1045.4 %all-gather.3.cloned.1.call-start = ((), (), s32[]{:S(2)}) async-start(), calls=%async_computation.1 | async-start | bytes 6389760 | tf_op jit(solution)/shard_map/all_gather | solution.py:18
  926.3 273.9 %all-gather.5.cloned.1.call-start = ((), (), s32[]{:S(2)}) async-start(), calls=%async_computation.3 | async-start | bytes 6389760 | tf_op jit(solution)/shard_map/all_gather | solution.py:39
Sparse Core Ops, SparseCore 0:
  16.4 832.9 reduce-scatter.1
  926.5 135.2 all-gather.2
  1066.6 133.6 all-gather.4
where the time goes:
time: 1210 us
  waiting for transfers between devices  1100 us (91%)
  blocking collectives  72.7 us (6%)
  between operations  14.5 us (1%)
  matrix products  13.6 us (1%)
    reduce_scatter x1, waiting for transfers between devices, on_device(): grad = lax.psum_scatter(partial_term, 'dp', scatter_dimension=0, tiled=True)  833 us
    all_gather x1, waiting for transfers between devices, on_device(): lax.all_gather(weight, 'dp', axis=0, tiled=True)  135 us
    all_gather x1, waiting for transfers between devices, on_device(): weight_next = lax.all_gather(shard_next, 'dp', axis=0, tiled=True)  133 us
    psum x1, blocking collectives, on_device(): total = lax.psum(local_squares, ('dp', 'tensor'))  72.7 us
  transfers between devices with their start and end apart: 3, of which 3 were waited for; matrix products, arithmetic and copies ran while one was open for 0% of the time, Pallas kernels for 0%

commit v1 on v0

--- a/solution.py
+++ b/solution.py
@@ -2,9 +2,16 @@
 import jax.numpy as jnp
 from jax import lax
 from jax.sharding import PartitionSpec as P
+from jax.lax import all_to_all, psum
 
 D = 3072
 FF = 4096
+
+
+def build_digits(array_here, device_axis):
+    return jnp.concatenate(
+        all_to_all(jnp.stack(psum(1, device_axis) * [array_here]), device_axis, 0, 0), axis=0
+    )
 
 
 def on_device(d_out, gate, up_proj, master, moment_one, moment_two):
@@ -36,7 +43,7 @@
         moment_one_next / (jnp.sqrt(moment_two_next) + 1e-08) + 0.1 * master
     )
     shard_next = master_next.astype(jnp.bfloat16)
-    weight_next = lax.all_gather(shard_next, "dp", axis=0, tiled=True)
+    weight_next = build_digits(shard_next, "dp")
     return (gate_grad, up_grad, master_next, moment_one_next, moment_two_next, weight_next)
 
 

time: 1210 us -> 1140 us (0.942)
  waiting for transfers between devices: 1100 us -> 1010 us
    all_to_all x0 -> x1, waiting for transfers between devices: none -> 151 us  [build_digits(): all_to_all(jnp.stack(psum(1, device_axis) * [array_here]), device_axis, 0...]
    all_gather x1 -> x0, waiting for transfers between devices: 133 us -> none  [on_device(): weight_next = lax.all_gather(shard_next, 'dp', axis=0, tiled=True)]
    all_gather x1, waiting for transfers between devices: 135 us -> 26 us  [on_device(): lax.all_gather(weight, 'dp', axis=0, tiled=True)]
where the time goes in v1:
time: 1140 us
  waiting for transfers between devices  1010 us (89%)
  blocking collectives  72.7 us (6%)
  between operations  14.8 us (1%)
  matrix products  13.6 us (1%)
    reduce_scatter x1, waiting for transfers between devices, on_device(): grad = lax.psum_scatter(partial_term, 'dp', scatter_dimension=0, tiled=True)  833 us
    all_to_all x1, waiting for transfers between devices, build_digits(): all_to_all(jnp.stack(psum(1, device_axis) * [array_here]), device_axis, 0...  151 us
    psum x1, blocking collectives, on_device(): total = lax.psum(local_squares, ('dp', 'tensor'))  72.7 us
    all_gather x1, waiting for transfers between devices, on_device(): lax.all_gather(weight, 'dp', axis=0, tiled=True)  26 us
  transfers between devices with their start and end apart: 3, of which 3 were waited for; matrix products, arithmetic and copies ran while one was open for 0% of the time, Pallas kernels for 0%

profile of v1, /device:TPU:2, one launch (start us, length us, event | category | flops | bytes accessed | tf_op | source)
XLA Modules:
  0.0 1136.5 jit_solution(1216332437341925912)
XLA Ops:
  7.2 0.0 copy-start
  7.2 0.0 reduce-scatter.2.cloned.1.call-start
  7.2 1.4 copy-done
  8.6 7.7 fusion.8
  16.3 0.0 copy-start.3
  16.3 0.0 copy-start.4
  16.3 0.0 copy-start.5
  16.3 0.0 reduce-scatter.2.cloned.1.call-update
  16.3 833.2 %reduce-scatter.2.cloned.1.call-done = f32[16,3072]{1,0:T(8,128)} async-done(((f32[1024,3072]{1,0:T(8,128)}), f32[16,3072]{1,0:T(8,128)}) %reduce-scatter.2.cloned.1.call-update) | async-done | bytes 196624 | tf_op jit(solution)/shard_map/reduce_scatter | solution.py:32
  849.5 1.6 multiply_reduce_fusion
  851.0 72.7 %psum.7 = f32[]{:T(128)} all-reduce(f32[]{:T(128)} %multiply_reduce_fusion), channel_id=1, replica_groups=mesh['dp'=64,'tensor'=4] {'dp','tensor'}, use_global_device_ids=true, to_apply=%region_2.3 | all-reduce | flops 1 | bytes 8 | tf_op jit(solution)/shard_map/psum | solution.py:37
  924.4 0.0 copy-done.3
  924.4 0.0 copy-done.4
  924.4 0.0 copy-done.5
  924.4 1.8 fusion.12
  926.3 3.5 stack.2
  929.8 0.0 copy-start.1
  929.8 0.0 copy-start.2
  929.8 10.0 all-to-all-start
  939.8 0.0 all-gather.2.cloned.1.call-start
  939.8 0.7 all-gather.2.cloned.1.call-update
  940.5 151.3 %all-to-all-done = bf16[64,16,3072]{2,1,0:T(8,128)(2,1)} async-done(((bf16[64,16,3072]{2,1,0:T(8,128)(2,1)}), bf16[64,16,3072]{2,1,0:T(8,128)(2,1)}, u32[]{:S(2)}, u32[]{:S(2)}) %all-to-all-start) | async-done | bytes 6291488 | tf_op jit(solution)/shard_map/all_to_all | solution.py:13
  1091.8 26.0 %all-gather.2.cloned.1.call-done = bf16[1024,3072]{1,0:T(8,128)(2,1)} async-done(((bf16[16,3072]{1,0:T(8,128)(2,1)}), bf16[1024,3072]{1,0:T(8,128)(2,1)}) %all-gather.2.cloned.1.call-update) | async-done | bytes 6291472 | tf_op jit(solution)/shard_map/all_gather | solution.py:25
  1117.8 0.0 copy-done.1
  1117.8 0.0 copy-done.2
  1117.8 5.9 multiply_convert_fusion
  1123.7 5.9 copy.13
Async XLA Ops:
  7.2 1.4 copy-start
  7.2 842.3 %reduce-scatter.2.cloned.1.call-start = ((), (), s32[]{:S(2)}) async-start(), calls=%async_computation.3 | async-start | bytes 12779520 | tf_op jit(solution)/shard_map/reduce_scatter | solution.py:32
  16.3 908.1 %copy-start.3 = (f32[16,3072]{1,0:T(8,128)S(1)}, f32[16,3072]{1,0:T(8,128)}, u32[]{:S(2)}) copy-start(f32[16,3072]{1,0:T(8,128)} %param.9) | copy-start | bytes 589828
  16.3 908.1 %copy-start.4 = (f32[16,3072]{1,0:T(8,128)S(1)}, f32[16,3072]{1,0:T(8,128)}, u32[]{:S(2)}) copy-start(f32[16,3072]{1,0:T(8,128)} %param.11) | copy-start | bytes 589828
  16.3 908.2 %copy-start.5 = (f32[16,3072]{1,0:T(8,128)S(1)}, f32[16,3072]{1,0:T(8,128)}, u32[]{:S(2)}) copy-start(f32[16,3072]{1,0:T(8,128)} %param.10) | copy-start | bytes 589828
  929.8 188.1 %copy-start.1 = (bf16[256,1024]{1,0:T(8,128)(2,1)S(1)}, bf16[256,1024]{1,0:T(8,128)(2,1)}, u32[]{:S(2)}) copy-start(bf16[256,1024]{1,0:T(8,128)(2,1)} %param.7) | copy-start | bytes 1572868
  929.8 188.1 %copy-start.2 = (bf16[256,1024]{1,0:T(8,128)(2,1)S(1)}, bf16[256,1024]{1,0:T(8,128)(2,1)}, u32[]{:S(2)}) copy-start(bf16[256,1024]{1,0:T(8,128)(2,1)} %param.8) | copy-start | bytes 1572868
  929.8 162.0 %all-to-all-start = ((bf16[64,16,3072]{2,1,0:T(8,128)(2,1)}), bf16[64,16,3072]{2,1,0:T(8,128)(2,1)}, u32[]{:S(2)}, u32[]{:S(2)}) async-start(bf16[64,16,3072]{2,1,0:T(8,128)(2,1)} %stack.2), calls=%async_computation.1 | async-start | bytes 12582912 | tf_op jit(solution)/shard_map/all_to_all | solution.py:13
  939.8 178.0 %all-gather.2.cloned.1.call-start = ((), (), s32[]{:S(2)}) async-start(), calls=%async_computation.2 | async-start | bytes 6389760 | tf_op jit(solution)/shard_map/all_gather | solution.py:25
Sparse Core Ops, SparseCore 0:
  16.4 832.9 reduce-scatter.1
  945.5 172.3 all-gather.1
